TPU v7x, 32 devices: a whole 2x2x4 slice. The times are simulated.
32 devices in a mesh: slab: 8 (over y, x, core), angle: 4 (over z).
Axes of the slice: x: 2, y: 2, z: 4, core: 2. Of those that a mesh axis runs over, the one named last changes fastest.
Arguments:
- volume: float32 [2048, 1024], P('slab'), may hold values from 0.25 to 2
- system: bfloat16 [4, 1024, 2048], P('angle'), as said below
- measured: bfloat16 [4, 2048, 2048], P('angle', 'slab'), as said below
- band_weight: bfloat16 [4, 4, 2048], P(None, 'angle', 'slab'), may hold values from 0.25 to 1
- band_offset: int32 [4, 2048], P('angle', 'slab'), may hold values from 0 to 2044, as said below
- row_first: int32 [4, 8], P('angle'), may hold values from 0 to 1789, as said below
- row_count: int32 [4, 8], P('angle'), may hold values from 259 to 512, as said below
Outputs:
- updated: float32 [2048, 1024], P('slab')
Inputs may be any that keep to these rules, and one draw needn't show every extreme that they name: `row_count`: every slab's window holds at most 512 rows; at every angle some slab's window holds exactly 512. row_first[a, s] = min(max(s * 256 + 256 // 2 - row_count[a, s] // 2, 0), 2048 - row_count[a, s]). `band_offset`: slice i of slab s starts its band at row_first[a, s] + (i (row_count[a, s] - 4)) // 255, so its 4 rows lie inside the slab's window. `system`: entries are nonnegative, and at every angle each pixel has positive entries. `measured`: entries are positive.
All inputs are finite; a program needn't handle non-finite values.
Results may differ from a plain program's by a relative error of at most 0.0003.
Values may be sent and summed in bfloat16 or wider, within the bound.
A program may use at most 64 MiB of HBM per device.

v0:
```python
import jax
import jax.numpy as jnp
from jax import lax
from jax.sharding import PartitionSpec as P

PIXROWS = 8
PIXCOLS = 128


SMOOTHING = 0.5
TV_STEP = 0.2
FLOOR = 0.5


def padded(cells, sides, width):
    for axis, dim in sides:
        count = lax.axis_size(axis)
        ends = count - 1
        head = lax.slice_in_dim(cells, 0, width, axis=dim)
        tail = lax.slice_in_dim(cells, cells.shape[dim] - width, cells.shape[dim], axis=dim)
        cells = jnp.concatenate(
            [
                lax.ppermute(tail, axis, [(i, (i + 1) % count) for i in range(ends)]),
                cells,
                lax.ppermute(head, axis, [((i + 1) % count, i) for i in range(ends)]),
            ],
            axis=dim,
        )
    return cells


def smooth_slope(differ):
    return differ / jnp.sqrt(differ * differ + SMOOTHING * SMOOTHING)


def band_matrix(weights, offsets, starts, counts, width):
    columns = jnp.arange(width, dtype=jnp.int32)
    relative = (offsets - starts)[:, None]
    matrix = jnp.zeros((offsets.shape[0], width), jnp.float32)
    for band_row in range(weights.shape[0]):
        matrix = matrix + weights[band_row][:, None] * (
            relative + band_row == columns[None, :]
        ).astype(jnp.float32)
    return matrix * (columns < counts).astype(jnp.float32)[None, :]


def plane_gradient(planes):
    gradient = jnp.zeros(planes.shape, jnp.float32)
    for axis_id in (1, 2):
        slopes = smooth_slope(jnp.diff(planes, axis=axis_id))
        before = [(0, 0), (0, 0), (0, 0)]
        after = [(0, 0), (0, 0), (0, 0)]
        before[axis_id] = (1, 0)
        after[axis_id] = (0, 1)
        gradient = gradient + jnp.pad(slopes, before) - jnp.pad(slopes, after)
    return gradient


def body(volume, system, measured, band_weight, band_offset, row_first, row_count):
    slices = volume.shape[0]
    detector = system.shape[2]
    nslab = lax.axis_size("slab")
    width = 2 * slices
    depth = slices * nslab
    my_slab = lax.axis_index("slab")
    matrix = system[0]
    starts_all = row_first[0]
    counts_all = row_count[0]
    my_start = starts_all[my_slab]
    my_count = counts_all[my_slab]
    weights = band_weight[:, 0, :].astype(jnp.float32)
    bands = band_matrix(weights, band_offset[0], my_start, my_count, width)
    bands_b = bands.astype(jnp.bfloat16)
    weight_total = jnp.sum(weights, axis=0)
    pixel_sums = jnp.sum(matrix, axis=1, dtype=jnp.float32)
    column_sums = jnp.sum(matrix, axis=0, dtype=jnp.float32)
    line = jnp.dot(volume.astype(jnp.bfloat16), matrix, preferred_element_type=jnp.float32).astype(
        jnp.bfloat16
    )
    window_rows = lax.dot_general(
        bands,
        line.astype(jnp.float32),
        (((0,), (0,)), ((), ())),
        precision=lax.Precision.HIGHEST,
        preferred_element_type=jnp.float32,
    )
    window_weight = jnp.sum(bands, axis=0)
    slots = width // nslab
    shift_out = my_start % nslab
    outgoing = jnp.roll(window_rows.reshape(slots, nslab, detector), shift_out, axis=1)
    outgoing_weight = jnp.roll(window_weight.reshape(slots, nslab), shift_out, axis=1)
    incoming, incoming_weight = (
        lax.all_to_all(outgoing, "slab", split_axis=1, concat_axis=1, tiled=True),
        lax.all_to_all(outgoing_weight, "slab", split_axis=1, concat_axis=1, tiled=True),
    )
    slot_index = jnp.arange(slots, dtype=jnp.int32)[:, None]
    paired_rows = starts_all[None, :] + slot_index * nslab + (my_slab - starts_all[None, :]) % nslab
    local_rows = jnp.arange(slices, dtype=jnp.int32)
    selector = paired_rows[None, :, :] // nslab == local_rows[:, None, None]
    forward = jnp.dot(
        selector.reshape(slices, slots * nslab).astype(jnp.float32),
        incoming.reshape(slots * nslab, detector),
        precision=lax.Precision.HIGHEST,
        preferred_element_type=jnp.float32,
    )
    row_weight = jnp.sum(
        jnp.where(selector, incoming_weight[None, :, :], jnp.float32(0.0)), axis=(1, 2)
    )
    scaled = (
        (measured[0].astype(jnp.float32) - forward)
        / jnp.maximum(row_weight[:, None] * column_sums[None, :], FLOOR)
    ).astype(jnp.bfloat16)
    valid = paired_rows < depth
    picked = scaled[jnp.minimum(paired_rows // nslab, slices - 1)]
    outgoing_back = jnp.where(valid[:, :, None], picked, jnp.zeros((), jnp.bfloat16))
    returned = lax.all_to_all(outgoing_back, "slab", split_axis=1, concat_axis=1, tiled=True)
    window = jnp.roll(returned, (nslab - shift_out) % nslab, axis=1).reshape(width, detector)
    spread = jnp.dot(bands_b, window, preferred_element_type=jnp.float32).astype(jnp.bfloat16)
    back = lax.dot_general(
        spread, matrix, (((1,), (1,)), ((), ())), preferred_element_type=jnp.float32
    )
    back_total, col_weight = lax.psum((back, weight_total[:, None] * pixel_sums[None, :]), "angle")
    middle = volume + back_total / col_weight
    extended = padded(middle, (("slab", 0),), 1)
    pair_lower = my_slab * slices + jnp.arange(slices + 1, dtype=jnp.int32) - 1
    keep_pair = (pair_lower >= 0) & (pair_lower + 1 <= depth - 1)
    slopes = jnp.where(
        keep_pair[:, None], smooth_slope(extended[1:] - extended[:-1]), jnp.float32(0.0)
    )
    across = slopes[:-1] - slopes[1:]
    inplane = plane_gradient(middle.reshape(slices, PIXROWS, PIXCOLS)).reshape(
        slices, PIXROWS * PIXCOLS
    )
    return middle - TV_STEP * (across + inplane)


def solution(mesh):
    return jax.shard_map(
        body,
        mesh=mesh,
        in_specs=(
            P("slab", None),
            P("angle", None, None),
            P("angle", "slab", None),
            P(None, "angle", "slab"),
            P("angle", "slab"),
            P("angle", None),
            P("angle", None),
        ),
        out_specs=P("slab", None),
        check_vma=False,
    )
```

profile of v0, /device:TPU:1, one launch (start us, length us, event | category | flops | bytes accessed | tf_op | source)
XLA Modules:
  0.0 239.3 jit_solution(11240814776169881554)
XLA Ops:
  6.5 1.3 constant_dynamic-slice_fusion
  9.7 1.3 broadcast_subtract_fusion
  11.7 0.8 fusion.76
  13.6 5.2 %all-to-all-start.1 = ((f32[64,8,1]{0,2,1:T(1,128)}), f32[64,8,1]{0,2,1:T(1,128)S(1)}, u32[]{:S(2)}, u32[]{:S(2)}) async-start(f32[64,8,1]{0,2,1:T(1,128)} %bitcast.14), calls=%async_computation.1 | async-start | bytes 8192 | tf_op jit(solution)/shard_map/all_to_all | solution.py:94
  18.8 3.8 %fusion.6 = bf16[256,2048]{1,0:T(8,128)(2,1)S(1)} fusion(bf16[1,1024,2048]{2,1,0:T(8,128)(2,1)} %param.8, f32[256,1024]{1,0:T(8,128)} %param.7), kind=kOutput, calls=%fused_computation.16 | convolution fusion | flops 1074528256 | bytes 6291456 | tf_op jit(solution)/shard_map/dot_general | solution.py:77
  22.6 2.2 convolution_bitcast_fusion
  24.8 2.4 %copy.35 = f32[64,8,2048]{2,0,1:T(8,128)S(1)} copy(f32[64,8,2048]{2,1,0:T(8,128)S(1)} %convolution_bitcast_fusion) | data formatting | bytes 8388608 | tf_op jit(solution)/shard_map/reshape | solution.py:90
  27.3 2.9 %fusion = f32[64,8,2048]{2,0,1:T(8,128)} fusion(s32[]{:T(128)S(6)} %select_n.98, f32[64,8,2048]{2,0,1:T(8,128)S(1)} %copy.35), kind=kLoop, calls=%fused_computation.5 | loop fusion | flops 1048576 | bytes 8388612 | tf_op jit(solution)/shard_map/jit(_roll_dynamic)/concatenate | solution.py:90
  30.2 4.8 %all-to-all-start = ((f32[64,8,2048]{2,0,1:T(8,128)}), f32[64,8,2048]{2,0,1:T(8,128)}, u32[]{:S(2)}, u32[]{:S(2)}) async-start(f32[64,8,2048]{2,0,1:T(8,128)} %fusion), calls=%async_computation | async-start | bytes 8388608 | tf_op jit(solution)/shard_map/all_to_all | solution.py:93
  35.4 3.7 %convert_reduce_fusion = (f32[1024]{0:T(1024)S(1)}, f32[2048]{0:T(1024)S(1)}) fusion(bf16[1,1024,2048]{2,1,0:T(8,128)(2,1)} %param.8), kind=kLoop, calls=%fused_computation.1 | loop fusion | flops 6288384 | bytes 4206592 | tf_op jit(solution)/shard_map/reduce_sum | solution.py:75
  39.3 41.3 %all-to-all-done = f32[64,8,2048]{2,0,1:T(8,128)} async-done(((f32[64,8,2048]{2,0,1:T(8,128)}), f32[64,8,2048]{2,0,1:T(8,128)}, u32[]{:S(2)}, u32[]{:S(2)}) %all-to-all-start) | async-done | bytes 4194336 | tf_op jit(solution)/shard_map/all_to_all | solution.py:93
  80.6 4.9 %fusion.10 = bf16[256,2048]{1,0:T(8,128)(2,1)S(1)} fusion(f32[64,8,2048]{2,0,1:T(8,128)} %all-to-all-done, bf16[1,256,2048]{2,1,0:T(8,128)(2,1)S(1)} %copy-done.3, f32[2048]{0:T(1024)S(1)} %get-tuple-element.6, f32[256]{0:T(256)S(1)} %select_reduce_fusion, s32[64,8]{0,1:T(8,128)S(1)} %add_select_fusion.1), kind=kOutput, calls=%fused_computation.18 | convolution fusion | flops 3224502272 | bytes 6302720 | tf_op jit(solution)/shard_map/dot_general | solution.py:100
  85.5 2.5 %gather_fusion = bf16[512,2048]{1,0:T(8,128)(2,1)S(1)} fusion(bf16[256,2048]{1,0:T(8,128)(2,1)S(1)} %fusion.10, s32[1024]{0:T(1024)S(1)} %pad_clamp_fusion), kind=kCustom, calls=%fused_computation | custom fusion | bytes 4196352 | tf_op jit(solution)/shard_map/gather | solution.py:114
  88.0 3.8 %copy_select_fusion = bf16[64,8,2048]{2,0,1:T(8,128)(2,1)} fusion(bf16[64,8,2048]{2,1,0:T(8,128)(2,1)S(1)} %bitcast.58, pred[64,8]{0,1:T(8,128)(4,1)S(1)} %fusion.61), kind=kLoop, calls=%fused_computation.21 | loop fusion | flops 1048576 | bytes 4194816 | tf_op jit(solution)/shard_map/jit(_where)/select_n | solution.py:115
  91.8 7.2 %all-to-all-start.2 = ((bf16[64,8,2048]{2,0,1:T(8,128)(2,1)}), bf16[64,8,2048]{2,0,1:T(8,128)(2,1)S(1)}, u32[]{:S(2)}, u32[]{:S(2)}) async-start(bf16[64,8,2048]{2,0,1:T(8,128)(2,1)} %copy_select_fusion), calls=%async_computation.2 | async-start | bytes 4194304 | tf_op jit(solution)/shard_map/all_to_all | solution.py:116
  99.0 1.1 broadcast_multiply_fusion
  100.2 22.0 %all-to-all-done.2 = bf16[64,8,2048]{2,0,1:T(8,128)(2,1)S(1)} async-done(((bf16[64,8,2048]{2,0,1:T(8,128)(2,1)}), bf16[64,8,2048]{2,0,1:T(8,128)(2,1)S(1)}, u32[]{:S(2)}, u32[]{:S(2)}) %all-to-all-start.2) | async-done | bytes 2097184 | tf_op jit(solution)/shard_map/all_to_all | solution.py:116
  122.1 2.5 %copy.41 = bf16[64,8,2048]{2,1,0:T(8,128)(2,1)} copy(bf16[64,8,2048]{2,0,1:T(8,128)(2,1)S(1)} %all-to-all-done.2) | data formatting | bytes 4194304 | tf_op jit(solution)/shard_map/all_to_all | solution.py:116
  124.6 7.0 %fusion.1 = f32[256,1024]{1,0:T(8,128)} fusion(bf16[1,1024,2048]{2,1,0:T(8,128)(2,1)} %param.8, s32[]{:T(128)S(6)} %select_n.105, bf16[64,8,2048]{2,1,0:T(8,128)(2,1)} %copy.41, f32[512]{0:T(512)S(1)} %fusion.67, f32[256]{0:T(256)S(1)} %bitcast.75, s32[256]{0:T(256)S(1)} %get-tuple-element.16, f32[256]{0:T(256)S(1)} %bitcast.72, ...), kind=kOutput, calls=%fused_computation.8 | convolution fusion | flops 1617035264 | bytes 7350276 | tf_op jit(solution)/shard_map/dot_general | solution.py:119
  131.6 90.1 %all-reduce.7.cloned.1.call-done = (f32[256,1024]{1,0:T(8,128)}, f32[256,1024]{1,0:T(8,128)}) async-done(((f32[256,1024]{1,0:T(8,128)}, f32[256,1024]{1,0:T(8,128)}), (f32[256,1024]{1,0:T(8,128)}, f32[256,1024]{1,0:T(8,128)})) %all-reduce.7.cloned.1.call-update) | async-done | bytes 2097168 | tf_op jit(solution)/shard_map/psum | solution.py:122
  221.7 1.8 divide_add_fusion
  224.4 2.6 %collective-permute-start = (f32[1,1024]{1,0:T(1,128)S(1)}, f32[1,1024]{1,0:T(1,128)S(1)}, u32[]{:S(2)}, u32[]{:S(2)}) collective-permute-start(f32[1,1024]{1,0:T(1,128)S(1)} %get-tuple-element.9), channel_id=1, source_target_pairs={{4,0},{8,4},{12,8},{16,12},{20,16},{24,20},{28,24},{5,1},{9,5},{13... | collective-permute-start | bytes 12296 | tf_op jit(solution)/shard_map/ppermute | solution.py:25
  227.0 3.0 %collective-permute-start.1 = (f32[1,1024]{1,0:T(1,128)S(1)}, f32[1,1024]{1,0:T(1,128)S(1)}, u32[]{:S(2)}, u32[]{:S(2)}) collective-permute-start(f32[1,1024]{1,0:T(1,128)S(1)} %get-tuple-element.10), channel_id=1, source_target_pairs={{0,4},{4,8},{8,12},{12,16},{16,20},{20,24},{24,28},{1,5},{5,9},{9,... | collective-permute-start | bytes 12296 | tf_op jit(solution)/shard_map/ppermute | solution.py:23
  231.0 1.5 fusion.15
  (35 shorter events, 4.2 us)
Async XLA Ops:
  13.6 16.6 %all-to-all-start.1 = ((f32[64,8,1]{0,2,1:T(1,128)}), f32[64,8,1]{0,2,1:T(1,128)S(1)}, u32[]{:S(2)}, u32[]{:S(2)}) async-start(f32[64,8,1]{0,2,1:T(1,128)} %bitcast.14), calls=%async_computation.1 | async-start | bytes 8192 | tf_op jit(solution)/shard_map/all_to_all | solution.py:94
  30.2 4.8 %copy-start.2 = (s32[1,8]{1,0:T(1,128)S(1)}, s32[1,8]{1,0:T(1,128)}, u32[]{:S(2)}) copy-start(s32[1,8]{1,0:T(1,128)} %param.12) | copy-start | bytes 100
  30.2 50.4 %all-to-all-start = ((f32[64,8,2048]{2,0,1:T(8,128)}), f32[64,8,2048]{2,0,1:T(8,128)}, u32[]{:S(2)}, u32[]{:S(2)}) async-start(f32[64,8,2048]{2,0,1:T(8,128)} %fusion), calls=%async_computation | async-start | bytes 8388608 | tf_op jit(solution)/shard_map/all_to_all | solution.py:93
  35.4 45.2 %copy-start.3 = (bf16[1,256,2048]{2,1,0:T(8,128)(2,1)S(1)}, bf16[1,256,2048]{2,1,0:T(8,128)(2,1)}, u32[]{:S(2)}) copy-start(bf16[1,256,2048]{2,1,0:T(8,128)(2,1)} %param.9) | copy-start | bytes 3145732
  91.8 7.2 %copy-start.1 = (bf16[4,1,256]{2,0,1:T(4,128)(2,1)S(1)}, bf16[4,1,256]{2,0,1:T(4,128)(2,1)}, u32[]{:S(2)}) copy-start(bf16[4,1,256]{2,0,1:T(4,128)(2,1)} %param.10) | copy-start | bytes 6148
  91.8 30.4 %all-to-all-start.2 = ((bf16[64,8,2048]{2,0,1:T(8,128)(2,1)}), bf16[64,8,2048]{2,0,1:T(8,128)(2,1)S(1)}, u32[]{:S(2)}, u32[]{:S(2)}) async-start(bf16[64,8,2048]{2,0,1:T(8,128)(2,1)} %copy_select_fusion), calls=%async_computation.2 | async-start | bytes 4194304 | tf_op jit(solution)/shard_map/all_to_all | solution.py:116
  99.0 122.7 %all-reduce.7.cloned.1.call-start = ((), (), s32[]{:S(2)}) async-start(), calls=%async_computation.3 | async-start | bytes 4194304 | tf_op jit(solution)/shard_map/psum | solution.py:122
  131.6 90.1 %copy-start = (f32[256,1024]{1,0:T(8,128)S(1)}, f32[256,1024]{1,0:T(8,128)}, u32[]{:S(2)}) copy-start(f32[256,1024]{1,0:T(8,128)} %param.7) | copy-start | bytes 3145732
  224.4 6.0 %collective-permute-start = (f32[1,1024]{1,0:T(1,128)S(1)}, f32[1,1024]{1,0:T(1,128)S(1)}, u32[]{:S(2)}, u32[]{:S(2)}) collective-permute-start(f32[1,1024]{1,0:T(1,128)S(1)} %get-tuple-element.9), channel_id=1, source_target_pairs={{4,0},{8,4},{12,8},{16,12},{20,16},{24,20},{28,24},{5,1},{9,5},{13... | collective-permute-start | bytes 12296 | tf_op jit(solution)/shard_map/ppermute | solution.py:25
  227.0 3.7 %collective-permute-start.1 = (f32[1,1024]{1,0:T(1,128)S(1)}, f32[1,1024]{1,0:T(1,128)S(1)}, u32[]{:S(2)}, u32[]{:S(2)}) collective-permute-start(f32[1,1024]{1,0:T(1,128)S(1)} %get-tuple-element.10), channel_id=1, source_target_pairs={{0,4},{4,8},{8,12},{12,16},{16,20},{20,24},{24,28},{1,5},{5,9},{9,... | collective-permute-start | bytes 12296 | tf_op jit(solution)/shard_map/ppermute | solution.py:23
Sparse Core Ops, SparseCore 0:
  131.7 89.9 all-reduce.6
where the time goes:
time: 241 us; the launch traced here: 239 us
  waiting for transfers between devices  154 us (64%)
  starting transfers between devices  22.8 us (9%)
  other arithmetic  19.5 us (8%)
  matrix products  17.9 us (7%)
  between operations  15.5 us (6%)
  local copies, waits for them, and re-layouts  9.94 us (4%)
    psum x1, waiting for transfers between devices, body(): lax.psum((back, weight_total[:, None] * pixel_sums[None, :]), 'angle')  90.1 us
    all_to_all x1, waiting for transfers between devices, body(): lax.all_to_all(outgoing, 'slab', split_axis=1, concat_axis=1, tiled=True)  41.3 us
    all_to_all x1, waiting for transfers between devices, body(): lax.all_to_all(outgoing_back, 'slab', split_axis=1, concat_axis=1, tiled=...  22 us
    all_to_all x1, starting transfers between devices, body(): lax.all_to_all(outgoing_back, 'slab', split_axis=1, concat_axis=1, tiled=...  7.22 us
    dot_general x1, matrix products, body(): lax.dot_general(spread, matrix, (((1,), (1,)), ((), ())), preferred_eleme...  6.97 us
    all_to_all x1, starting transfers between devices, body(): lax.all_to_all(outgoing_weight, 'slab', split_axis=1, concat_axis=1, tile...  5.22 us
    dot_general x1, matrix products, body(): jnp.dot(selector.reshape(slices, slots * nslab).astype(jnp.float32), inco...  4.91 us
  transfers between devices with their start and end apart: 6, of which 4 were waited for; matrix products, arithmetic and copies ran while one was open for 7% of the time, Pallas kernels for 0%

commit v1 on v0

v1 whole, which is shorter than its diff:
```python
import functools

import jax
import jax.numpy as jnp
from jax import lax
from jax.experimental import pallas as pl
from jax.experimental.pallas import tpu as pltpu
from jax.sharding import PartitionSpec as P

SMOOTHING = 0.5
TV_STEP = 0.2
FLOOR = 0.5
TILE = 512
FAR = 128
LANES = 128


def smooth_slope(differ):
    return differ * lax.rsqrt(differ * differ + SMOOTHING * SMOOTHING)


def kernel(
    n, m, vol_ref, small_ref, sys_ref, meas_ref, out_ref,
    sysv, volx, smallx, win, fwd, inv, spread, band_t, band_own, col_sum, pack, packs,
    acc, recv_a, recv_b, total, mid, edge_lo, edge_hi, halo_prev, halo_next,
    sys_sem, own_sem, vol_send, vol_recv, small_send, small_recv, win_send, win_recv,
    pack_send, pack_recv, a_send, a_recv, b_send, b_recv, edge_send, edge_recv,
):
    me = lax.axis_index("slab")
    ang = lax.axis_index("angle")
    slices, pixels = vol_ref.shape
    detector = sysv.shape[1]
    width = 2 * slices
    chunks = pixels // LANES
    half = m // 2
    f32, bf16 = jnp.float32, jnp.bfloat16

    def slab_peer(k):
        return lax.rem(me + k, n)

    def angle_peer(k):
        return lax.rem(ang + k, m)

    def first_block(slab):
        return jnp.clip(2 * slab - 1, 0, 2 * n - 4)

    def remote(src, dst, send, recv, axis, peer):
        return pltpu.make_async_remote_copy(
            src_ref=src, dst_ref=dst, send_sem=send, recv_sem=recv,
            device_id={axis: peer}, device_id_type=pl.DeviceIdType.MESH,
        )

    barrier = pltpu.get_barrier_semaphore()
    for k in range(1, n):
        pl.semaphore_signal(barrier, inc=1, device_id={"slab": slab_peer(k)},
                            device_id_type=pl.DeviceIdType.MESH)
    for k in range(1, m):
        pl.semaphore_signal(barrier, inc=1, device_id={"angle": angle_peer(k)},
                            device_id_type=pl.DeviceIdType.MESH)
    sys_copy = pltpu.make_async_copy(sys_ref, sysv, sys_sem)
    sys_copy.start()
    own_copy = pltpu.make_async_copy(meas_ref.at[pl.ds(first_block(me), 4)], win.at[me], own_sem)
    own_copy.start()
    own = pl.ds(0, slices)
    volx[own, :] = vol_ref[...].astype(bf16)
    smallx[:, own] = small_ref[...]
    has_prev, has_next = me > 0, me < n - 1
    prev_at, next_at, far_at = slices, 2 * slices, 3 * slices
    far_up = jnp.logical_or(me == 0, me == n - 3)
    far_down = jnp.logical_or(me == 2, me == n - 1)
    has_far = jnp.logical_or(far_up, far_down)

    def clear(start, size):
        volx[pl.ds(start, size), :] = jnp.zeros((size, pixels), bf16)
        smallx[:, pl.ds(start, size)] = jnp.zeros((8, size), f32)

    @pl.when(jnp.logical_not(has_prev))
    def _():
        clear(prev_at, slices)

    @pl.when(jnp.logical_not(has_next))
    def _():
        clear(next_at, slices)

    @pl.when(jnp.logical_not(has_far))
    def _():
        clear(far_at, FAR)

    pl.semaphore_wait(barrier, n + m - 2)

    def halo(slot, src_at, dst_at, size, peer):
        return (
            remote(smallx.at[:, pl.ds(src_at, size)], smallx.at[:, pl.ds(dst_at, size)],
                   small_send.at[slot], small_recv.at[slot], "slab", peer),
            remote(volx.at[pl.ds(src_at, size)], volx.at[pl.ds(dst_at, size)],
                   vol_send.at[slot], vol_recv.at[slot], "slab", peer),
        )

    to_next = halo(0, 0, prev_at, slices, lax.rem(me + 1, n))
    to_prev = halo(1, 0, next_at, slices, lax.rem(me + n - 1, n))
    to_up = halo(2, slices - FAR, far_at, FAR, lax.rem(me + 2, n))
    to_down = halo(2, 0, far_at, FAR, lax.rem(me + n - 2, n))
    moves = ((has_next, to_next), (has_prev, to_prev), (far_up, to_up), (far_down, to_down))
    arrivals = ((has_prev, to_next), (has_next, to_prev), (has_far, to_up))
    for condition, copies in moves:
        @pl.when(condition)
        def _():
            for copy in copies:
                copy.start()

    shares = []
    for k in range(1, n):
        peer = slab_peer(k)
        shares.append(remote(meas_ref.at[pl.ds(first_block(peer), 4)], win.at[me],
                             win_send.at[k], win_recv.at[k], "slab", peer))
    for copy in shares:
        copy.start()

    sys_copy.wait()
    col_sum[...] = jnp.dot(jnp.ones((8, pixels), bf16), sysv[...], preferred_element_type=f32)
    pixel_sum = lax.dot_general(jnp.ones((8, detector), bf16), sysv[...],
                                (((1,), (1,)), ((), ())), preferred_element_type=f32)
    keep = lax.broadcasted_iota(jnp.int32, (8, 1), 0) == 0
    pack[:, pl.ds(0, pixels)] = jnp.where(keep, pixel_sum, 0.0)
    weight_total = jnp.sum(small_ref[0:4, :], axis=0, keepdims=True)
    pack[:, pl.ds(pixels, slices)] = jnp.where(keep, weight_total, 0.0)
    packs[pl.ds(ang, 1)] = pack[...][None]
    pack_copies = [
        remote(pack, packs.at[ang], pack_send.at[k], pack_recv.at[k], "angle", angle_peer(k))
        for k in range(1, m)
    ]
    for copy in pack_copies:
        copy.start()

    for condition, copies in arrivals:
        @pl.when(condition)
        def _():
            for copy in copies:
                copy.wait_recv()

    share = width // n
    position = lax.broadcasted_iota(jnp.int32, (width, 1), 0)
    source = lax.shift_right_logical(position, share.bit_length() - 1)
    row = first_block(me) * (slices // 2) + lax.bitwise_and(position, share - 1) * n + source
    row = row.astype(f32)
    row_weight = jnp.zeros((width, 1), f32)
    for start in range(0, volx.shape[0], FAR):
        at = pl.ds(start, FAR)
        behind = row - smallx[4:5, at]
        block = jnp.zeros((width, FAR), f32)
        for k in range(4):
            block = jnp.where(behind == float(k), smallx[k : k + 1, at], block)
        row_weight = row_weight + jnp.sum(block, axis=1, keepdims=True)
        band_t[:, at] = block.astype(bf16)
        if start < slices:
            band_own[at, :] = block.T.astype(bf16)

    @pl.loop(0, detector // TILE)
    def _(step):
        at = pl.ds(pl.multiple_of(step * TILE, TILE), TILE)
        line = jnp.dot(volx[...], sysv[:, at], preferred_element_type=f32).astype(bf16)
        fwd[:, at] = jnp.dot(band_t[...], line, preferred_element_type=f32)
        inv[:, at] = 1.0 / jnp.maximum(row_weight * col_sum[0:1, at], FLOOR)

    own_copy.wait()
    for copy in shares:
        copy.wait_recv()

    @pl.loop(0, detector // TILE)
    def _(step):
        at = pl.ds(pl.multiple_of(step * TILE, TILE), TILE)
        rows = win[:, :, :, at].astype(f32).reshape(width, TILE)
        residual = ((rows - fwd[:, at]) * inv[:, at]).astype(bf16)
        spread[:, at] = jnp.dot(band_own[...], residual, preferred_element_type=f32).astype(bf16)

    for copy in pack_copies:
        copy.wait_recv()

    left = ang < half
    inner = jnp.where(left, ang + 1, ang - 1)
    outer = jnp.where(left, jnp.maximum(ang - 1, 0), jnp.minimum(ang + 1, m - 1))
    centre = jnp.logical_or(ang == half - 1, ang == half)
    has_outer = jnp.logical_and(ang > 0, ang < m - 1)
    not_centre = jnp.logical_not(centre)
    no_outer = jnp.logical_not(has_outer)

    def up_copy(c, target):
        sem = a_recv if target is recv_a else b_recv
        return remote(acc.at[c], target.at[c], a_send.at[c], sem.at[c], "angle", inner)

    def down_copy(c):
        return remote(total.at[c], recv_b.at[c], b_send.at[c], b_recv.at[c], "angle", outer)

    def multiply(pair):
        product = lax.dot_general(spread[...], sysv[pl.ds(pair * 2 * LANES, 2 * LANES), :],
                                  (((1,), (1,)), ((), ())), preferred_element_type=f32)
        acc[2 * pair] = product[:, :LANES]
        acc[2 * pair + 1] = product[:, LANES:]

    def collect(c):
        @pl.when(has_outer)
        def _():
            up_copy(c, recv_a).wait_recv()
            acc[c] = acc[c] + recv_a[c]

        @pl.when(centre)
        def _():
            up_copy(c, recv_b).start()

        @pl.when(not_centre)
        def _():
            up_copy(c, recv_a).start()

    all_packs = packs[...].reshape(m * 8, pixels + slices)

    def finish(c):
        down_copy(c).wait_recv()
        at = pl.ds(c * LANES, LANES)
        whole = jnp.where(centre, acc[c] + recv_b[c], recv_b[c])
        total[c] = whole

        @pl.when(has_outer)
        def _():
            down_copy(c).start()

        weight = lax.dot_general(
            all_packs[:, pixels:], all_packs[:, c * LANES : (c + 1) * LANES],
            (((0,), (0,)), ((), ())), precision=lax.Precision.HIGHEST, preferred_element_type=f32,
        )
        cells = vol_ref[:, at] + whole / weight
        mid[c] = cells
        edge_lo[c : c + 1, :] = cells[0:1, :]
        edge_hi[c : c + 1, :] = cells[slices - 1 : slices, :]

    def run(lag):
        for c in range(chunks + lag):
            if c < chunks:
                if c % 2 == 0:
                    multiply(c // 2)
                collect(c)
            if c >= lag:
                finish(c - lag)

    @pl.when(has_outer)
    def _():
        run(2)

    @pl.when(no_outer)
    def _():
        run(chunks)

    edge_up = remote(edge_hi, halo_prev, edge_send.at[0], edge_recv.at[0], "slab", lax.rem(me + 1, n))
    edge_down = remote(edge_lo, halo_next, edge_send.at[1], edge_recv.at[1], "slab", lax.rem(me + n - 1, n))

    @pl.when(has_next)
    def _():
        edge_up.start()

    @pl.when(has_prev)
    def _():
        edge_down.start()

    @pl.when(jnp.logical_not(has_prev))
    def _():
        halo_prev[...] = edge_lo[...]

    @pl.when(jnp.logical_not(has_next))
    def _():
        halo_next[...] = edge_hi[...]

    lane = lax.broadcasted_iota(jnp.int32, (1, LANES), 1)
    below = None
    for c in range(chunks):
        cells = mid[c]
        slope = jnp.where(lane < LANES - 1,
                          smooth_slope(pltpu.roll(cells, LANES - 1, axis=1) - cells), 0.0)
        gradient = pltpu.roll(slope, 1, axis=1) - slope
        if below is not None:
            gradient = gradient + below
        if c + 1 < chunks:
            below = smooth_slope(mid[c + 1] - cells)
            gradient = gradient - below
        total_at = pl.ds(c * LANES, LANES)
        out_ref[:, total_at] = gradient

    @pl.when(has_prev)
    def _():
        edge_up.wait_recv()

    @pl.when(has_next)
    def _():
        edge_down.wait_recv()

    for c in range(chunks):
        at = pl.ds(c * LANES, LANES)
        cells = mid[c]
        upper = jnp.concatenate([cells[1:, :], halo_next[c : c + 1, :]], axis=0)
        slope = smooth_slope(upper - cells)
        first = smooth_slope(cells[0:1, :] - halo_prev[c : c + 1, :])
        lower = jnp.concatenate([first, slope[: slices - 1, :]], axis=0)
        out_ref[:, at] = cells - TV_STEP * (out_ref[:, at] + lower - slope)

    for condition, copies in moves:
        @pl.when(condition)
        def _():
            for copy in copies:
                copy.wait_send()
    for copy in shares + pack_copies:
        copy.wait_send()
    for c in range(chunks):
        up_copy(c, recv_a).wait_send()

        @pl.when(has_outer)
        def _():
            down_copy(c).wait_send()

    @pl.when(has_next)
    def _():
        edge_up.wait_send()

    @pl.when(has_prev)
    def _():
        edge_down.wait_send()


def body(n, m, volume, system, measured, band_weight, band_offset, row_first, row_count):
    slices, pixels = volume.shape
    detector = system.shape[2]
    grain = slices // 2 // n
    width = 2 * slices
    chunks = pixels // LANES
    extended = 3 * slices + FAR
    small = jnp.concatenate(
        [
            band_weight[:, 0, :].astype(jnp.float32),
            band_offset.astype(jnp.float32),
            jnp.zeros((3, slices), jnp.float32),
        ],
        axis=0,
    )
    f32, bf16 = jnp.float32, jnp.bfloat16
    dma = pltpu.SemaphoreType.DMA
    chunk = pltpu.VMEM((chunks, slices, LANES), f32)
    edge = pltpu.VMEM((chunks, LANES), f32)
    vmem = pl.BlockSpec(memory_space=pltpu.VMEM)
    return pl.pallas_call(
        functools.partial(kernel, n, m),
        out_shape=jax.ShapeDtypeStruct((slices, pixels), f32),
        in_specs=[vmem, vmem, pl.BlockSpec(memory_space=pl.ANY), pl.BlockSpec(memory_space=pl.ANY)],
        out_specs=vmem,
        scratch_shapes=[
            pltpu.VMEM((pixels, detector), bf16),
            pltpu.VMEM((extended, pixels), bf16),
            pltpu.VMEM((8, extended), f32),
            pltpu.VMEM((n, 4, grain, detector), bf16),
            pltpu.VMEM((width, detector), f32),
            pltpu.VMEM((width, detector), f32),
            pltpu.VMEM((slices, detector), bf16),
            pltpu.VMEM((width, extended), bf16),
            pltpu.VMEM((slices, width), bf16),
            pltpu.VMEM((8, detector), f32),
            pltpu.VMEM((8, pixels + slices), f32),
            pltpu.VMEM((m, 8, pixels + slices), f32),
            chunk, chunk, chunk, chunk, chunk,
            edge, edge, edge, edge,
            dma, dma,
            dma((3,)), dma((3,)), dma((3,)), dma((3,)), dma((n,)), dma((n,)),
            dma((m,)), dma((m,)),
            dma((chunks,)), dma((chunks,)), dma((chunks,)), dma((chunks,)),
            dma((2,)), dma((2,)),
        ],
        compiler_params=pltpu.CompilerParams(
            collective_id=0, has_side_effects=True, vmem_limit_bytes=56 * 1024 * 1024
        ),
    )(volume, small, system[0], measured[0].reshape(2 * n, grain, detector))


def solution(mesh):
    return jax.shard_map(
        functools.partial(body, mesh.shape["slab"], mesh.shape["angle"]),
        mesh=mesh,
        in_specs=(
            P("slab", None),
            P("angle", None, None),
            P("angle", "slab", None),
            P(None, "angle", "slab"),
            P("angle", "slab"),
            P("angle", None),
            P("angle", None),
        ),
        out_specs=P("slab", None),
        check_vma=False,
    )
```

time: 241 us -> 87.6 us (0.36)
  waiting for transfers between devices: 154 us -> 0 us
  Pallas kernels: 0 us -> 82.8 us
  starting transfers between devices: 22.8 us -> 0 us
  matrix products: 17.9 us -> 0 us
  other arithmetic: 19.5 us -> 2.03 us
  between operations: 15.5 us -> 0.01 us
  local copies, waits for them, and re-layouts: 9.94 us -> 2.39 us
    psum x1 -> x0, waiting for transfers between devices: 90.1 us -> none  [body(): lax.psum((back, weight_total[:, None] * pixel_sums[None, :]), 'angle')]
    pallas_call x0 -> x1, Pallas kernels: none -> 82.8 us  [body(): pl.pallas_call(functools.partial(kernel, n, m), out_shape=jax.ShapeDtypeS...]
    all_to_all x3 -> x0, waiting for transfers between devices: 63.3 us -> none  [the longest x1 41.3 us: body(): lax.all_to_all(outgoing, 'slab', split_axis=1, concat_axis=1, tiled=True)]
    dot_general x4 -> x0, matrix products: 17.9 us -> none  [the longest x1 6.97 us: body(): lax.dot_general(spread, matrix, (((1,), (1,)), ((), ())), preferred_eleme...]
    all_to_all x3 -> x0, starting transfers between devices: 17.3 us -> none  [the longest x1 7.22 us: body(): lax.all_to_all(outgoing_back, 'slab', split_axis=1, concat_axis=1, tiled=...]
    ppermute x2 -> x0, starting transfers between devices: 5.58 us -> none  [the longest x1 3.01 us: padded(): lax.ppermute(tail, axis, [(i, (i + 1) % count) for i in range(ends)])]
    reduce_sum x4 -> x0, other arithmetic: 4.28 us -> none  [the longest x1 3.69 us: body(): pixel_sums = jnp.sum(matrix, axis=1, dtype=jnp.float32)]
    select_n x4 -> x0, other arithmetic: 4.25 us -> none  [the longest x1 3.77 us: body(): jnp.where(valid[:, :, None], picked, jnp.zeros((), jnp.bfloat16))]
  transfers between devices with their start and end apart: 6 -> 0, of which waited for: 4 -> 0; matrix products, arithmetic and copies ran while one was open for 7% -> 0% of each run, Pallas kernels for 0% -> 0%
where the time goes in v1:
time: 87.6 us; the launch traced here: 87.2 us
  Pallas kernels  82.8 us (95%)
  local copies, waits for them, and re-layouts  2.39 us (3%)
  other arithmetic  2.03 us (2%)
    pallas_call x1, Pallas kernels, body(): pl.pallas_call(functools.partial(kernel, n, m), out_shape=jax.ShapeDtypeS...  82.8 us
    unnamed x1, local copies, waits for them, and re-layouts  2.31 us

profile of v1, /device:TPU:1, one launch (start us, length us, event | category | flops | bytes accessed | tf_op | source)
XLA Modules:
  0.0 87.2 jit_solution(14780438539957092313)
XLA Ops:
  0.0 0.1 pad.2.clone
  0.1 0.7 convert_element_type.11
  0.8 0.7 bitcast_convert_fusion
  1.4 0.7 maximum_maximum_fusion.small_ref
  2.1 82.8 %shard_map.55 = f32[256,1024]{1,0:T(8,128)} custom-call(f32[256,1024]{1,0:T(8,128)} %vol_ref.1, f32[8,256]{1,0:T(8,128)} %maximum_maximum_fusion.small_ref, bf16[1024,2048]{1,0:T(8,128)(2,1)} %bitcast.5, bf16[16,16,2048]{2,1,0:T(8,128)(2,1)} %bitcast.6), custom_call_target="tpu_custom_call" | custom-call | tf_op jit(solution)/shard_map/pallas_call | solution.py:346
  84.9 2.3 %copy.7 = f32[256,1024]{1,0:T(8,128)} copy(f32[256,1024]{1,0:T(8,128)} %shard_map.55) | data formatting | bytes 2097152
  (1 shorter events, 0.0 us)

commit v2 on v1

--- a/solution.py
+++ b/solution.py
@@ -12,6 +12,9 @@
 FLOOR = 0.5
 TILE = 512
 FAR = 128
+NEAR_ROWS = 144
+FAR_ROWS = 80
+PARTS = 2
 LANES = 128
 
 
@@ -24,7 +27,7 @@
     sysv, volx, smallx, win, fwd, inv, spread, band_t, band_own, col_sum, pack, packs,
     acc, recv_a, recv_b, total, mid, edge_lo, edge_hi, halo_prev, halo_next,
     sys_sem, own_sem, vol_send, vol_recv, small_send, small_recv, win_send, win_recv,
-    pack_send, pack_recv, a_send, a_recv, b_send, b_recv, edge_send, edge_recv,
+    relay_send, relay_recv, pack_send, pack_recv, a_send, a_recv, b_send, b_recv, edge_send, edge_recv,
 ):
     me = lax.axis_index("slab")
     ang = lax.axis_index("angle")
@@ -32,7 +35,10 @@
     detector = sysv.shape[1]
     width = 2 * slices
     chunks = pixels // LANES
+    piece = slices // PARTS
     half = m // 2
+    chip, core = me // 2, lax.rem(me, 2)
+    partner = chip * 2 + 1 - core
     f32, bf16 = jnp.float32, jnp.bfloat16
 
     def slab_peer(k):
@@ -50,6 +56,9 @@
             device_id={axis: peer}, device_id_type=pl.DeviceIdType.MESH,
         )
 
+    extra = volx.shape[0] - slices
+    volx[pl.ds(slices, extra), :] = jnp.zeros((extra, pixels), bf16)
+    smallx[:, pl.ds(slices, extra)] = jnp.zeros((8, extra), f32)
     barrier = pltpu.get_barrier_semaphore()
     for k in range(1, n):
         pl.semaphore_signal(barrier, inc=1, device_id={"slab": slab_peer(k)},
@@ -70,50 +79,79 @@
     far_down = jnp.logical_or(me == 2, me == n - 1)
     has_far = jnp.logical_or(far_up, far_down)
 
-    def clear(start, size):
-        volx[pl.ds(start, size), :] = jnp.zeros((size, pixels), bf16)
-        smallx[:, pl.ds(start, size)] = jnp.zeros((8, size), f32)
-
-    @pl.when(jnp.logical_not(has_prev))
-    def _():
-        clear(prev_at, slices)
-
-    @pl.when(jnp.logical_not(has_next))
-    def _():
-        clear(next_at, slices)
-
-    @pl.when(jnp.logical_not(has_far))
-    def _():
-        clear(far_at, FAR)
-
     pl.semaphore_wait(barrier, n + m - 2)
 
-    def halo(slot, src_at, dst_at, size, peer):
+    def halo(slot, src_at, dst_at, size, src_row, dst_row, rows, peer):
         return (
             remote(smallx.at[:, pl.ds(src_at, size)], smallx.at[:, pl.ds(dst_at, size)],
                    small_send.at[slot], small_recv.at[slot], "slab", peer),
-            remote(volx.at[pl.ds(src_at, size)], volx.at[pl.ds(dst_at, size)],
+            remote(volx.at[pl.ds(src_row, rows)], volx.at[pl.ds(dst_row, rows)],
                    vol_send.at[slot], vol_recv.at[slot], "slab", peer),
         )
 
-    to_next = halo(0, 0, prev_at, slices, lax.rem(me + 1, n))
-    to_prev = halo(1, 0, next_at, slices, lax.rem(me + n - 1, n))
-    to_up = halo(2, slices - FAR, far_at, FAR, lax.rem(me + 2, n))
-    to_down = halo(2, 0, far_at, FAR, lax.rem(me + n - 2, n))
-    moves = ((has_next, to_next), (has_prev, to_prev), (far_up, to_up), (far_down, to_down))
-    arrivals = ((has_prev, to_next), (has_next, to_prev), (has_far, to_up))
+    above, under = lax.rem(me + 1, n), lax.rem(me + n - 1, n)
+    cut = slices - NEAR_ROWS
+    next_all = halo(0, 0, prev_at, slices, 0, prev_at, slices, above)
+    next_part = halo(0, 0, prev_at, slices, cut, prev_at + cut, NEAR_ROWS, above)
+    prev_all = halo(1, 0, next_at, slices, 0, next_at, slices, under)
+    prev_part = halo(1, 0, next_at, slices, 0, next_at, NEAR_ROWS, under)
+    far_cut = FAR - FAR_ROWS
+    to_up = halo(2, slices - FAR, far_at, FAR, slices - FAR_ROWS, far_at + far_cut, FAR_ROWS,
+                 lax.rem(me + 2, n))
+    to_down = halo(2, 0, far_at, FAR, 0, far_at, FAR_ROWS, lax.rem(me + n - 2, n))
+    both, either, no = jnp.logical_and, jnp.logical_or, jnp.logical_not
+    send_up_all = either(me == 0, me == n - 2)
+    send_down_all = either(me == n - 1, me == 1)
+    get_prev_all = either(me == 1, me == n - 1)
+    get_next_all = either(me == n - 2, me == 0)
+    moves = (
+        (both(has_next, send_up_all), next_all),
+        (both(has_next, no(send_up_all)), next_part),
+        (both(has_prev, send_down_all), prev_all),
+        (both(has_prev, no(send_down_all)), prev_part),
+        (far_up, to_up),
+        (far_down, to_down),
+    )
+    arrivals = (
+        (both(has_prev, get_prev_all), next_all),
+        (both(has_prev, no(get_prev_all)), next_part),
+        (both(has_next, get_next_all), prev_all),
+        (both(has_next, no(get_next_all)), prev_part),
+        (far_down, to_up),
+        (far_up, to_down),
+    )
     for condition, copies in moves:
         @pl.when(condition)
         def _():
             for copy in copies:
                 copy.start()
 
-    shares = []
-    for k in range(1, n):
-        peer = slab_peer(k)
-        shares.append(remote(meas_ref.at[pl.ds(first_block(peer), 4)], win.at[me],
-                             win_send.at[k], win_recv.at[k], "slab", peer))
-    for copy in shares:
+    chips = n // 2
+    shares, gets, relays, relay_gets = [], [], [], []
+    shift = first_block(chip * 2 + 1) - first_block(chip * 2)
+    relay_from = jnp.where(core == 0, shift, 3 - shift)
+    for d in range(1, chips):
+        for e in range(2):
+            slot = 2 * d + e
+            peer = lax.rem(chip + d, chips) * 2 + e
+            shares.append(remote(
+                meas_ref.at[pl.ds(first_block(peer) + e, 3)], win.at[me, pl.ds(e, 3)],
+                win_send.at[slot], win_recv.at[2 * d + core], "slab", peer))
+            source = lax.rem(chip + chips - d, chips) * 2 + e
+            gets.append(remote(
+                meas_ref.at[pl.ds(0, 3)], win.at[source, pl.ds(core, 3)],
+                win_send.at[slot], win_recv.at[slot], "slab", peer))
+            relays.append(remote(
+                win.at[source, pl.ds(relay_from, 1)], win.at[source, pl.ds(3 * core, 1)],
+                relay_send.at[slot], relay_recv.at[slot], "slab", partner))
+            relay_gets.append(remote(
+                win.at[source, pl.ds(relay_from, 1)], win.at[source, pl.ds(3 - 3 * core, 1)],
+                relay_send.at[slot], relay_recv.at[slot], "slab", partner))
+    beside = remote(meas_ref.at[pl.ds(first_block(partner), 4)], win.at[me],
+                    win_send.at[0], win_recv.at[0], "slab", partner)
+    beside_get = remote(meas_ref.at[pl.ds(0, 4)], win.at[partner],
+                        win_send.at[0], win_recv.at[0], "slab", partner)
+    for copy in shares + [beside]:
         copy.start()
 
     sys_copy.wait()
@@ -163,8 +201,12 @@
         inv[:, at] = 1.0 / jnp.maximum(row_weight * col_sum[0:1, at], FLOOR)
 
     own_copy.wait()
-    for copy in shares:
-        copy.wait_recv()
+    for get, relay in zip(gets, relays):
+        get.wait_recv()
+        relay.start()
+    beside_get.wait_recv()
+    for get in relay_gets:
+        get.wait_recv()
 
     @pl.loop(0, detector // TILE)
     def _(step):
@@ -194,8 +236,11 @@
     def multiply(pair):
         product = lax.dot_general(spread[...], sysv[pl.ds(pair * 2 * LANES, 2 * LANES), :],
                                   (((1,), (1,)), ((), ())), preferred_element_type=f32)
-        acc[2 * pair] = product[:, :LANES]
-        acc[2 * pair + 1] = product[:, LANES:]
+        for c in range(2):
+            for part in range(PARTS):
+                acc[(2 * pair + c) * PARTS + part] = product[
+                    part * piece : (part + 1) * piece, c * LANES : (c + 1) * LANES
+                ]
 
     def collect(c):
         @pl.when(has_outer)
@@ -213,33 +258,40 @@
 
     all_packs = packs[...].reshape(m * 8, pixels + slices)
 
-    def finish(c):
-        down_copy(c).wait_recv()
-        at = pl.ds(c * LANES, LANES)
-        whole = jnp.where(centre, acc[c] + recv_b[c], recv_b[c])
-        total[c] = whole
+    def finish(index):
+        down_copy(index).wait_recv()
+        c, part = index // PARTS, index % PARTS
+        first = part * piece
+        whole = jnp.where(centre, acc[index] + recv_b[index], recv_b[index])
+        total[index] = whole
 
         @pl.when(has_outer)
         def _():
-            down_copy(c).start()
+            down_copy(index).start()
 
         weight = lax.dot_general(
-            all_packs[:, pixels:], all_packs[:, c * LANES : (c + 1) * LANES],
+            all_packs[:, pixels + first : pixels + first + piece],
+            all_packs[:, c * LANES : (c + 1) * LANES],
             (((0,), (0,)), ((), ())), precision=lax.Precision.HIGHEST, preferred_element_type=f32,
         )
-        cells = vol_ref[:, at] + whole / weight
-        mid[c] = cells
-        edge_lo[c : c + 1, :] = cells[0:1, :]
-        edge_hi[c : c + 1, :] = cells[slices - 1 : slices, :]
+        rows = pl.ds(first, piece)
+        cells = vol_ref[rows, pl.ds(c * LANES, LANES)] + whole / weight
+        mid[c, rows] = cells
+        if part == 0:
+            edge_lo[c : c + 1, :] = cells[0:1, :]
+        if part == PARTS - 1:
+            edge_hi[c : c + 1, :] = cells[piece - 1 : piece, :]
+
+    pieces = chunks * PARTS
 
     def run(lag):
-        for c in range(chunks + lag):
-            if c < chunks:
-                if c % 2 == 0:
-                    multiply(c // 2)
-                collect(c)
-            if c >= lag:
-                finish(c - lag)
+        for index in range(pieces + lag):
+            if index < pieces:
+                if index % (2 * PARTS) == 0:
+                    multiply(index // (2 * PARTS))
+                collect(index)
+            if index >= lag:
+                finish(index - lag)
 
     @pl.when(has_outer)
     def _():
@@ -247,7 +299,7 @@
 
     @pl.when(no_outer)
     def _():
-        run(chunks)
+        run(pieces)
 
     edge_up = remote(edge_hi, halo_prev, edge_send.at[0], edge_recv.at[0], "slab", lax.rem(me + 1, n))
     edge_down = remote(edge_lo, halo_next, edge_send.at[1], edge_recv.at[1], "slab", lax.rem(me + n - 1, n))
@@ -305,9 +357,9 @@
         def _():
             for copy in copies:
                 copy.wait_send()
-    for copy in shares + pack_copies:
+    for copy in shares + [beside] + relays + pack_copies:
         copy.wait_send()
-    for c in range(chunks):
+    for c in range(pieces):
         up_copy(c, recv_a).wait_send()
 
         @pl.when(has_outer)
@@ -340,7 +392,7 @@
     )
     f32, bf16 = jnp.float32, jnp.bfloat16
     dma = pltpu.SemaphoreType.DMA
-    chunk = pltpu.VMEM((chunks, slices, LANES), f32)
+    chunk = pltpu.VMEM((chunks * PARTS, slices // PARTS, LANES), f32)
     edge = pltpu.VMEM((chunks, LANES), f32)
     vmem = pl.BlockSpec(memory_space=pltpu.VMEM)
     return pl.pallas_call(
@@ -361,12 +413,13 @@
             pltpu.VMEM((8, detector), f32),
             pltpu.VMEM((8, pixels + slices), f32),
             pltpu.VMEM((m, 8, pixels + slices), f32),
-            chunk, chunk, chunk, chunk, chunk,
+            chunk, chunk, chunk, chunk,
+            pltpu.VMEM((chunks, slices, LANES), f32),
             edge, edge, edge, edge,
             dma, dma,
             dma((3,)), dma((3,)), dma((3,)), dma((3,)), dma((n,)), dma((n,)),
-            dma((m,)), dma((m,)),
-            dma((chunks,)), dma((chunks,)), dma((chunks,)), dma((chunks,)),
+            dma((n,)), dma((n,)), dma((m,)), dma((m,)),
+            *[dma((chunks * PARTS,))] * 4,
             dma((2,)), dma((2,)),
         ],
         compiler_params=pltpu.CompilerParams(

time: 87.6 us -> 77.5 us (0.88)
  Pallas kernels: 82.8 us -> 72.9 us
    pallas_call x1, Pallas kernels: 82.8 us -> 72.9 us  [body(): pl.pallas_call(functools.partial(kernel, n, m), out_shape=jax.ShapeDtypeS...]
where the time goes in v2:
time: 77.5 us; the launch traced here: 77.3 us
  Pallas kernels  72.9 us (94%)
  local copies, waits for them, and re-layouts  2.39 us (3%)
  other arithmetic  2.03 us (3%)
    pallas_call x1, Pallas kernels, body(): pl.pallas_call(functools.partial(kernel, n, m), out_shape=jax.ShapeDtypeS...  72.9 us
    unnamed x1, local copies, waits for them, and re-layouts  2.31 us

profile of v2, /device:TPU:1, one launch (start us, length us, event | category | flops | bytes accessed | tf_op | source)
XLA Modules:
  0.0 77.3 jit_solution(9308946303957111236)
XLA Ops:
  0.0 0.1 pad.2.clone
  0.1 0.7 convert_element_type.11
  0.8 0.7 bitcast_convert_fusion
  1.4 0.7 maximum_maximum_fusion.small_ref
  2.1 72.9 %shard_map.55 = f32[256,1024]{1,0:T(8,128)} custom-call(f32[256,1024]{1,0:T(8,128)} %vol_ref.1, f32[8,256]{1,0:T(8,128)} %maximum_maximum_fusion.small_ref, bf16[1024,2048]{1,0:T(8,128)(2,1)} %bitcast.5, bf16[16,16,2048]{2,1,0:T(8,128)(2,1)} %bitcast.6), custom_call_target="tpu_custom_call" | custom-call | tf_op jit(solution)/shard_map/pallas_call | solution.py:398
  75.0 2.3 %copy.7 = f32[256,1024]{1,0:T(8,128)} copy(f32[256,1024]{1,0:T(8,128)} %shard_map.55) | data formatting | bytes 2097152
  (1 shorter events, 0.0 us)

commit v3 on v2

--- a/solution.py
+++ b/solution.py
@@ -25,7 +25,7 @@
 def kernel(
     n, m, vol_ref, small_ref, sys_ref, meas_ref, out_ref,
     sysv, volx, smallx, win, fwd, inv, spread, band_t, band_own, col_sum, pack, packs,
-    acc, recv_a, recv_b, total, mid, edge_lo, edge_hi, halo_prev, halo_next,
+    scale, acc, recv_a, recv_b, total, mid, edge_lo, edge_hi, halo_prev, halo_next,
     sys_sem, own_sem, vol_send, vol_recv, small_send, small_recv, win_send, win_recv,
     relay_send, relay_recv, pack_send, pack_recv, a_send, a_recv, b_send, b_recv, edge_send, edge_recv,
 ):
@@ -200,6 +200,17 @@
         fwd[:, at] = jnp.dot(band_t[...], line, preferred_element_type=f32)
         inv[:, at] = 1.0 / jnp.maximum(row_weight * col_sum[0:1, at], FLOOR)
 
+    for copy in pack_copies:
+        copy.wait_recv()
+    all_packs = packs[...].reshape(m * 8, pixels + slices)
+    for part in range(PARTS):
+        first = part * piece
+        weight = lax.dot_general(
+            all_packs[:, pixels + first : pixels + first + piece], all_packs[:, :pixels],
+            (((0,), (0,)), ((), ())), precision=lax.Precision.HIGHEST, preferred_element_type=f32,
+        )
+        scale[pl.ds(first, piece), :] = 1.0 / weight
+
     own_copy.wait()
     for get, relay in zip(gets, relays):
         get.wait_recv()
@@ -214,9 +225,6 @@
         rows = win[:, :, :, at].astype(f32).reshape(width, TILE)
         residual = ((rows - fwd[:, at]) * inv[:, at]).astype(bf16)
         spread[:, at] = jnp.dot(band_own[...], residual, preferred_element_type=f32).astype(bf16)
-
-    for copy in pack_copies:
-        copy.wait_recv()
 
     left = ang < half
     inner = jnp.where(left, ang + 1, ang - 1)
@@ -256,8 +264,6 @@
         def _():
             up_copy(c, recv_a).start()
 
-    all_packs = packs[...].reshape(m * 8, pixels + slices)
-
     def finish(index):
         down_copy(index).wait_recv()
         c, part = index // PARTS, index % PARTS
@@ -269,13 +275,9 @@
         def _():
             down_copy(index).start()
 
-        weight = lax.dot_general(
-            all_packs[:, pixels + first : pixels + first + piece],
-            all_packs[:, c * LANES : (c + 1) * LANES],
-            (((0,), (0,)), ((), ())), precision=lax.Precision.HIGHEST, preferred_element_type=f32,
-        )
         rows = pl.ds(first, piece)
-        cells = vol_ref[rows, pl.ds(c * LANES, LANES)] + whole / weight
+        at = pl.ds(c * LANES, LANES)
+        cells = vol_ref[rows, at] + whole * scale[rows, at]
         mid[c, rows] = cells
         if part == 0:
             edge_lo[c : c + 1, :] = cells[0:1, :]
@@ -413,6 +415,7 @@
             pltpu.VMEM((8, detector), f32),
             pltpu.VMEM((8, pixels + slices), f32),
             pltpu.VMEM((m, 8, pixels + slices), f32),
+            pltpu.VMEM((slices, pixels), f32),
             chunk, chunk, chunk, chunk,
             pltpu.VMEM((chunks, slices, LANES), f32),
             edge, edge, edge, edge,

time: 77.5 us -> 76.7 us (0.990)
  Pallas kernels: 72.9 us -> 72.1 us
    pallas_call x1, Pallas kernels: 72.9 us -> 72.1 us  [body(): pl.pallas_call(functools.partial(kernel, n, m), out_shape=jax.ShapeDtypeS...]
where the time goes in v3:
time: 76.7 us; the launch traced here: 76.5 us
  Pallas kernels  72.1 us (94%)
  local copies, waits for them, and re-layouts  2.39 us (3%)
  other arithmetic  2.03 us (3%)
    pallas_call x1, Pallas kernels, body(): pl.pallas_call(functools.partial(kernel, n, m), out_shape=jax.ShapeDtypeS...  72.1 us
    unnamed x1, local copies, waits for them, and re-layouts  2.31 us

profile of v3, /device:TPU:1, one launch (start us, length us, event | category | flops | bytes accessed | tf_op | source)
XLA Modules:
  0.0 76.5 jit_solution(12639684060602799351)
XLA Ops:
  0.0 0.1 pad.2.clone
  0.1 0.7 convert_element_type.11
  0.8 0.7 bitcast_convert_fusion
  1.4 0.7 maximum_maximum_fusion.small_ref
  2.1 72.1 %shard_map.55 = f32[256,1024]{1,0:T(8,128)} custom-call(f32[256,1024]{1,0:T(8,128)} %vol_ref.1, f32[8,256]{1,0:T(8,128)} %maximum_maximum_fusion.small_ref, bf16[1024,2048]{1,0:T(8,128)(2,1)} %bitcast.5, bf16[16,16,2048]{2,1,0:T(8,128)(2,1)} %bitcast.6), custom_call_target="tpu_custom_call" | custom-call | tf_op jit(solution)/shard_map/pallas_call | solution.py:400
  74.2 2.3 %copy.7 = f32[256,1024]{1,0:T(8,128)} copy(f32[256,1024]{1,0:T(8,128)} %shard_map.55) | data formatting | bytes 2097152
  (1 shorter events, 0.0 us)
